TPU v7x, 1024 devices: a whole 8x8x8 slice. The times are simulated.
1024 devices in a mesh: gx: 16 (over x, z_hi), gy: 8 (over z_lo, core), gz: 8 (over y).
Axes of the slice: x: 8, y: 8, z: 8 (z_hi: 2, z_lo: 4; z = z_hi * 4 + z_lo), core: 2. Of those that a mesh axis runs over, the one named last changes fastest.
Arguments:
- body_pos: float32 [3, 524288], P(None, ('gx', 'gy', 'gz')), may hold values from -1 to 1
- body_mass: float32 [524288], P(('gx', 'gy', 'gz')), may hold values from 0.003 to 0.03
- cell_mass: float32 [2097152], P(('gx', 'gy', 'gz')), may hold values from 0.003 to 0.03
- cell_center: float32 [3, 2097152], P(None, ('gx', 'gy', 'gz')), may hold values from -1 to 1
- cell_quad: float32 [6, 2097152], P(None, ('gx', 'gy', 'gz')), may hold values from -0.001 to 0.001
- cell_lists: int32 [1024, 5, 1024], P(('gx', 'gy', 'gz')), may hold values from 0 to 6143, as said below
- slot_masks: int32 [1024, 5, 1024], P(('gx', 'gy', 'gz')), may hold values from 0 to 1, as said below
- face_lists: int32 [1024, 2, 4], P(('gx', 'gy', 'gz')), may hold values from 0 to 3, as said below
- face_counts: int32 [1024, 2], P(('gx', 'gy', 'gz')), may hold values from 1 to 4
Outputs:
- accel: float32 [3, 524288], P(None, ('gx', 'gy', 'gz'))
Inputs may be any that keep to these rules, and one draw needn't show every extreme that they name: `cell_lists`: at level l (from 0) every entry is below 2048 + l * 1024, and the 1024 entries of one level of one domain are distinct. `slot_masks`: each level of each domain has exactly 768 ones. `face_lists`: each side's list of a domain is a permutation of its 4 blocks.
All inputs are finite; a program needn't handle non-finite values.
Results may differ from a plain program's by a relative error of at most 0.00002.
Values sent between devices are 32-bit elements; how exact they have to be, the bound alone decides.
A program may use at most 64 MiB of HBM per device.

v0:
```python
import math

import jax
import jax.numpy as jnp
from jax import lax
from jax.sharding import PartitionSpec as P

NBLK = 4
BLK = 128
LEVELS = 5


soften = 0.01


def padded(cells, sides, width):
    for axis, dim in sides:
        count = lax.axis_size(axis)
        ends = count - 1
        head = lax.slice_in_dim(cells, 0, width, axis=dim)
        tail = lax.slice_in_dim(cells, cells.shape[dim] - width, cells.shape[dim], axis=dim)
        cells = jnp.concatenate(
            [
                lax.ppermute(tail, axis, [(i, (i + 1) % count) for i in range(ends)]),
                cells,
                lax.ppermute(head, axis, [((i + 1) % count, i) for i in range(ends)]),
            ],
            axis=dim,
        )
    return cells


def swapped(value, axis, apart):
    mask = 2**apart
    pairs = [(source, source ^ mask) for source in range(lax.axis_size(axis))]
    return lax.ppermute(value, axis, pairs)


def tile_accel(targets, sources):
    offset = targets[:, :, None] - sources[1:4, None, :]
    distance = jnp.sum(offset * offset, axis=0) + soften
    inverse_one = lax.rsqrt(distance)
    inverse_two = inverse_one * inverse_one
    inverse_three = inverse_one * inverse_two
    radial = -sources[0][None, :] * inverse_three
    if sources.shape[0] == 10:
        quadrupole = sources[4:10]
        quad_x = (
            quadrupole[0][None, :] * offset[0]
            + quadrupole[3][None, :] * offset[1]
            + quadrupole[4][None, :] * offset[2]
        )
        quad_y = (
            quadrupole[3][None, :] * offset[0]
            + quadrupole[1][None, :] * offset[1]
            + quadrupole[5][None, :] * offset[2]
        )
        quad_z = (
            quadrupole[4][None, :] * offset[0]
            + quadrupole[5][None, :] * offset[1]
            + quadrupole[2][None, :] * offset[2]
        )
        inverse_five = inverse_three * inverse_two
        quad_form = offset[0] * quad_x + offset[1] * quad_y + offset[2] * quad_z
        radial = radial - 2.5 * quad_form * inverse_five * inverse_two
        return jnp.stack(
            [
                jnp.sum(radial * offset[0] + quad_x * inverse_five, axis=1),
                jnp.sum(radial * offset[1] + quad_y * inverse_five, axis=1),
                jnp.sum(radial * offset[2] + quad_z * inverse_five, axis=1),
            ]
        )
    return jnp.sum(radial[None] * offset, axis=2)


def tile_width_for(count):
    for width in (1024, 1152, 768, 512, 384, 256, 128):
        if count % width == 0:
            return width
    return math.gcd(count, 1024)


def cell_forces(targets, sources):
    source_count = sources.shape[1]
    source_width = tile_width_for(source_count)
    source_tiles = sources.reshape(
        sources.shape[0], source_count // source_width, source_width
    ).transpose(1, 0, 2)
    target_count = targets.shape[1]
    target_width = math.gcd(target_count, 512)
    target_tiles = targets.reshape(3, target_count // target_width, target_width).transpose(1, 0, 2)

    def one_target_tile(target_tile):

        def add_tile(summed, source_tile):
            return (summed + tile_accel(target_tile, source_tile), None)

        summed, unused = lax.scan(add_tile, jnp.zeros_like(target_tile), source_tiles)
        return summed

    results = lax.map(one_target_tile, target_tiles)
    return results.transpose(1, 0, 2).reshape(3, target_count)


def shards(
    body_pos,
    body_mass,
    cell_mass,
    cell_center,
    cell_quad,
    cell_lists,
    slot_masks,
    face_lists,
    face_counts,
):
    bit_count = lax.axis_size(("gx", "gy", "gz")).bit_length() - 1
    stacked = jnp.concatenate([body_mass[None], body_pos], 0)
    blocks_all = stacked.reshape(4, NBLK, BLK)
    chosen_blocks = jnp.take(blocks_all, face_lists[0].reshape(-1), axis=1)
    slot_numbers = jnp.arange(NBLK, dtype=jnp.int32)
    face_live = (slot_numbers[None, :] < face_counts[0][:, None]).reshape(-1)
    outgoing = chosen_blocks * face_live.astype(jnp.float32)[None, :, None]
    extended = padded(outgoing, (("gz", 1),), NBLK)
    near_bodies = jnp.concatenate(
        [stacked, extended[:, :NBLK].reshape(4, -1), extended[:, 3 * NBLK :].reshape(4, -1)], 1
    )
    held_cells = jnp.concatenate([cell_mass[None], cell_center, cell_quad], 0)
    force_blocks = [held_cells]
    forces = cell_forces(body_pos, near_bodies)
    for level_no in range(LEVELS):
        partner_bit = bit_count - 1 - level_no
        slot_index = cell_lists[0, level_no]
        slot_live = slot_masks[0, level_no]
        outbound = jnp.take(held_cells, slot_index, axis=1) * slot_live.astype(jnp.float32)[None]
        arrived = swapped(outbound, ("gx", "gy", "gz"), partner_bit)
        force_blocks.append(arrived)
        held_cells = jnp.concatenate([held_cells, arrived], 1)
    forces = forces + cell_forces(body_pos, held_cells)
    return forces


def solution(mesh):
    in_specs = (
        P(None, ("gx", "gy", "gz")),
        P(("gx", "gy", "gz")),
        P(("gx", "gy", "gz")),
        P(None, ("gx", "gy", "gz")),
        P(None, ("gx", "gy", "gz")),
        P(("gx", "gy", "gz"), None, None),
        P(("gx", "gy", "gz"), None, None),
        P(("gx", "gy", "gz"), None, None),
        P(("gx", "gy", "gz"), None),
    )
    out_specs = P(None, ("gx", "gy", "gz"))
    return jax.shard_map(shards, mesh=mesh, in_specs=in_specs, out_specs=out_specs, check_vma=False)
```

profile of v0, /device:TPU:48, one launch (start us, length us, event | category | flops | bytes accessed | tf_op | source)
XLA Modules:
  0.0 246.0 jit_solution(647891139125306291)
XLA Ops:
  6.8 4.8 %collective-permute-start = (f32[4,4,128]{2,0,1:T(4,128)S(1)}, f32[4,4,128]{2,0,1:T(4,128)S(1)}, u32[]{:S(2)}, u32[]{:S(2)}) collective-permute-start(f32[4,4,128]{2,0,1:T(4,128)S(1)} %get-tuple-element.150), channel_id=1, source_target_pairs={{0,1},{1,2},{2,3},{3,4},{4,5},{5,6},{6,7},{8,9},{9,10},{10,11},{11... | collective-permute-start | bytes 24584 | tf_op jit(solution)/shard_map/ppermute | solution.py:24
  18.2 7.4 %collective-permute-start.2 = (f32[10,1024]{0,1:T(8,128)S(1)}, f32[10,1024]{0,1:T(8,128)S(1)}, u32[]{:S(2)}, u32[]{:S(2)}) collective-permute-start(f32[10,1024]{0,1:T(8,128)S(1)} %multiply_bitcast_fusion.4), channel_id=1, source_target_pairs={{0,512},{1,513},{2,514},{3,515},{4,516},{5,517},{6,518},{7,519},{8... | collective-permute-start | bytes 122888 | tf_op jit(solution)/shard_map/ppermute | solution.py:36
  30.0 13.1 %collective-permute-done.2 = f32[10,1024]{0,1:T(8,128)S(1)} collective-permute-done((f32[10,1024]{0,1:T(8,128)S(1)}, f32[10,1024]{0,1:T(8,128)S(1)}, u32[]{:S(2)}, u32[]{:S(2)}) %collective-permute-start.2) | collective-permute-done | bytes 40992 | tf_op jit(solution)/shard_map/ppermute | solution.py:36
  43.3 4.0 %gather_fusion.2 = f32[1024,10]{1,0:T(8,128)} fusion(f32[10,3072]{0,1:T(8,128)S(1)} %pad_maximum_fusion.2, s32[1024]{0:T(1024)S(1)} %broadcast_clamp_fusion.3), kind=kCustom, calls=%fused_computation.2 | custom fusion | bytes 86016 | tf_op jit(solution)/shard_map/jit(_take)/gather | solution.py:134
  48.7 9.7 %collective-permute-start.3 = (f32[10,1024]{0,1:T(8,128)S(1)}, f32[10,1024]{0,1:T(8,128)S(1)}, u32[]{:S(2)}, u32[]{:S(2)}) collective-permute-start(f32[10,1024]{0,1:T(8,128)S(1)} %multiply_bitcast_fusion.3), channel_id=1, source_target_pairs={{0,256},{1,257},{2,258},{3,259},{4,260},{5,261},{6,262},{7,263},{8... | collective-permute-start | bytes 122888 | tf_op jit(solution)/shard_map/ppermute | solution.py:36
  59.5 21.7 %collective-permute-done.3 = f32[10,1024]{0,1:T(8,128)S(1)} collective-permute-done((f32[10,1024]{0,1:T(8,128)S(1)}, f32[10,1024]{0,1:T(8,128)S(1)}, u32[]{:S(2)}, u32[]{:S(2)}) %collective-permute-start.3) | collective-permute-done | bytes 40992 | tf_op jit(solution)/shard_map/ppermute | solution.py:36
  82.7 4.4 %gather_fusion.3 = f32[1024,10]{1,0:T(8,128)S(1)} fusion(f32[10,4096]{0,1:T(8,128)} %pad_maximum_fusion.1, s32[1024]{0:T(1024)S(1)} %broadcast_clamp_fusion.2), kind=kCustom, calls=%fused_computation.3 | custom fusion | bytes 86016 | tf_op jit(solution)/shard_map/jit(_take)/gather | solution.py:134
  91.2 13.0 %collective-permute-done.4 = f32[10,1024]{0,1:T(8,128)S(1)} collective-permute-done((f32[10,1024]{0,1:T(8,128)}, f32[10,1024]{0,1:T(8,128)S(1)}, u32[]{:S(2)}, u32[]{:S(2)}) %collective-permute-start.4) | collective-permute-done | bytes 40992 | tf_op jit(solution)/shard_map/ppermute | solution.py:36
  105.9 4.5 %gather_fusion.4 = f32[1024,10]{1,0:T(8,128)S(1)} fusion(f32[10,5120]{0,1:T(8,128)} %pad_maximum_fusion, s32[1024]{0:T(1024)S(1)} %broadcast_clamp_fusion.1), kind=kCustom, calls=%fused_computation.4 | custom fusion | bytes 86016 | tf_op jit(solution)/shard_map/jit(_take)/gather | solution.py:134
  110.8 14.6 %collective-permute-start.5 = (f32[10,1024]{0,1:T(8,128)S(1)}, f32[10,1024]{0,1:T(8,128)S(1)}, u32[]{:S(2)}, u32[]{:S(2)}) collective-permute-start(f32[10,1024]{0,1:T(8,128)S(1)} %multiply_bitcast_fusion.1), channel_id=1, source_target_pairs={{0,64},{1,65},{2,66},{3,67},{4,68},{5,69},{6,70},{7,71},{8,72},{9,... | collective-permute-start | bytes 122888 | tf_op jit(solution)/shard_map/ppermute | solution.py:36
  126.4 10.4 %collective-permute-done.5 = f32[10,1024]{0,1:T(8,128)S(1)} collective-permute-done((f32[10,1024]{0,1:T(8,128)S(1)}, f32[10,1024]{0,1:T(8,128)S(1)}, u32[]{:S(2)}, u32[]{:S(2)}) %collective-permute-start.5) | collective-permute-done | bytes 40992 | tf_op jit(solution)/shard_map/ppermute | solution.py:36
  137.6 4.7 %gather_fusion.5 = f32[1024,10]{1,0:T(8,128)S(1)} fusion(f32[10,6144]{0,1:T(8,128)} %constant_dynamic-update-slice_fusion, s32[1024]{0:T(1024)S(1)} %broadcast_clamp_fusion), kind=kCustom, calls=%fused_computation.5 | custom fusion | bytes 86016 | tf_op jit(solution)/shard_map/jit(_take)/gather | solution.py:134
  142.6 15.5 %collective-permute-start.6 = (f32[10,1024]{0,1:T(8,128)S(1)}, f32[10,1024]{0,1:T(8,128)S(1)}, u32[]{:S(2)}, u32[]{:S(2)}) collective-permute-start(f32[10,1024]{0,1:T(8,128)S(1)} %multiply_bitcast_fusion), channel_id=1, source_target_pairs={{0,32},{1,33},{2,34},{3,35},{4,36},{5,37},{6,38},{7,39},{8,40},{9,... | collective-permute-start | bytes 122888 | tf_op jit(solution)/shard_map/ppermute | solution.py:36
  158.3 23.0 %collective-permute-done.6 = f32[10,1024]{0,1:T(8,128)S(1)} collective-permute-done((f32[10,1024]{0,1:T(8,128)S(1)}, f32[10,1024]{0,1:T(8,128)S(1)}, u32[]{:S(2)}, u32[]{:S(2)}) %collective-permute-start.6) | collective-permute-done | bytes 40992 | tf_op jit(solution)/shard_map/ppermute | solution.py:36
  181.8 63.5 %while.37 = (s32[]{:T(128)}, f32[3,512]{1,0:T(4,128)S(1)}, f32[7,10,1024]{2,1,0:T(8,128)S(1)}, f32[3,512]{1,0:T(4,128)S(1)}, s32[]{:T(128)}, /*index=5*/s32[]{:T...) while((s32[]{:T(128)}, f32[3,512]{1,0:T(4,128)S(1)}, f32[7,10,1024]{2,1,0:T(8,128)S(1)}, ...), condition=%wide.region_9.10_spmd.clone, body=%wide.region_4.9_spmd.clone.sunk | while | flops 25695752 | bytes 16931076 | solution.py:98
  181.9 3.6 %broadcast_subtract_fusion.2 = (f32[3,512,1024]{2,1,0:T(8,128)}, f32[512,1024]{1,0:T(8,128)S(1)}) fusion(f32[3,1024]{1,0:T(4,128)S(1)} %dynamic-slice_bitcast_fusion.5, f32[3,512]{1,0:T(4,128)S(1)} %get-tuple-element.278), kind=kLoop, calls=%fused_computation.7.clone.2 | loop fusion | flops 4194304 | bytes 8407040 | tf_op jit(solution)/shard_map/while/body/eval_jaxpr/while/body/eval_jaxpr/sub | solution.py:40
  185.5 5.4 %add_reduce_fusion.4 = (f32[512]{0:T(512)S(1)}, f32[512]{0:T(512)S(1)}, f32[512]{0:T(512)S(1)}) fusion(f32[3,512,1024]{2,1,0:T(8,128)} %get-tuple-element.216, f32[1024]{0:T(1024)S(1)} %bitcast.134, f32[1024]{0:T(1024)S(1)} %bitcast.135, f32[1024]{0:T(1024)S(1)} %bitcast.136, f32[512,1024]{1,0:T(8,128)S(1)} %get-tuple-element.220, ...), kind=kLoop, calls=%fused_computation.18.clone.1 | loop fusion | flops 21494272 | bytes 8423424 | tf_op jit(solution)/shard_map/while/body/eval_jaxpr/while/body/eval_jaxpr/reduce_sum | solution.py:68
  190.9 3.6 %broadcast_subtract_fusion.2 = (f32[3,512,1024]{2,1,0:T(8,128)}, f32[512,1024]{1,0:T(8,128)S(1)}) fusion(f32[3,1024]{1,0:T(4,128)S(1)} %dynamic-slice_bitcast_fusion.5, f32[3,512]{1,0:T(4,128)S(1)} %get-tuple-element.278), kind=kLoop, calls=%fused_computation.7.clone.2 | loop fusion | flops 4194304 | bytes 8407040 | tf_op jit(solution)/shard_map/while/body/eval_jaxpr/while/body/eval_jaxpr/sub | solution.py:40
  194.6 5.4 %add_reduce_fusion.4 = (f32[512]{0:T(512)S(1)}, f32[512]{0:T(512)S(1)}, f32[512]{0:T(512)S(1)}) fusion(f32[3,512,1024]{2,1,0:T(8,128)} %get-tuple-element.216, f32[1024]{0:T(1024)S(1)} %bitcast.134, f32[1024]{0:T(1024)S(1)} %bitcast.135, f32[1024]{0:T(1024)S(1)} %bitcast.136, f32[512,1024]{1,0:T(8,128)S(1)} %get-tuple-element.220, ...), kind=kLoop, calls=%fused_computation.18.clone.1 | loop fusion | flops 21494272 | bytes 8423424 | tf_op jit(solution)/shard_map/while/body/eval_jaxpr/while/body/eval_jaxpr/reduce_sum | solution.py:68
  203.7 5.4 %add_reduce_fusion.4 = (f32[512]{0:T(512)S(1)}, f32[512]{0:T(512)S(1)}, f32[512]{0:T(512)S(1)}) fusion(f32[3,512,1024]{2,1,0:T(8,128)} %get-tuple-element.216, f32[1024]{0:T(1024)S(1)} %bitcast.134, f32[1024]{0:T(1024)S(1)} %bitcast.135, f32[1024]{0:T(1024)S(1)} %bitcast.136, f32[512,1024]{1,0:T(8,128)S(1)} %get-tuple-element.220, ...), kind=kLoop, calls=%fused_computation.18.clone.1 | loop fusion | flops 21494272 | bytes 8423424 | tf_op jit(solution)/shard_map/while/body/eval_jaxpr/while/body/eval_jaxpr/reduce_sum | solution.py:68
  212.7 5.4 %add_reduce_fusion.4 = (f32[512]{0:T(512)S(1)}, f32[512]{0:T(512)S(1)}, f32[512]{0:T(512)S(1)}) fusion(f32[3,512,1024]{2,1,0:T(8,128)} %get-tuple-element.216, f32[1024]{0:T(1024)S(1)} %bitcast.134, f32[1024]{0:T(1024)S(1)} %bitcast.135, f32[1024]{0:T(1024)S(1)} %bitcast.136, f32[512,1024]{1,0:T(8,128)S(1)} %get-tuple-element.220, ...), kind=kLoop, calls=%fused_computation.18.clone.1 | loop fusion | flops 21494272 | bytes 8423424 | tf_op jit(solution)/shard_map/while/body/eval_jaxpr/while/body/eval_jaxpr/reduce_sum | solution.py:68
  221.8 5.4 %add_reduce_fusion.4 = (f32[512]{0:T(512)S(1)}, f32[512]{0:T(512)S(1)}, f32[512]{0:T(512)S(1)}) fusion(f32[3,512,1024]{2,1,0:T(8,128)} %get-tuple-element.216, f32[1024]{0:T(1024)S(1)} %bitcast.134, f32[1024]{0:T(1024)S(1)} %bitcast.135, f32[1024]{0:T(1024)S(1)} %bitcast.136, f32[512,1024]{1,0:T(8,128)S(1)} %get-tuple-element.220, ...), kind=kLoop, calls=%fused_computation.18.clone.1 | loop fusion | flops 21494272 | bytes 8423424 | tf_op jit(solution)/shard_map/while/body/eval_jaxpr/while/body/eval_jaxpr/reduce_sum | solution.py:68
  230.9 5.4 %add_reduce_fusion.4 = (f32[512]{0:T(512)S(1)}, f32[512]{0:T(512)S(1)}, f32[512]{0:T(512)S(1)}) fusion(f32[3,512,1024]{2,1,0:T(8,128)} %get-tuple-element.216, f32[1024]{0:T(1024)S(1)} %bitcast.134, f32[1024]{0:T(1024)S(1)} %bitcast.135, f32[1024]{0:T(1024)S(1)} %bitcast.136, f32[512,1024]{1,0:T(8,128)S(1)} %get-tuple-element.220, ...), kind=kLoop, calls=%fused_computation.18.clone.1 | loop fusion | flops 21494272 | bytes 8423424 | tf_op jit(solution)/shard_map/while/body/eval_jaxpr/while/body/eval_jaxpr/reduce_sum | solution.py:68
  239.9 5.4 %add_reduce_fusion.4 = (f32[512]{0:T(512)S(1)}, f32[512]{0:T(512)S(1)}, f32[512]{0:T(512)S(1)}) fusion(f32[3,512,1024]{2,1,0:T(8,128)} %get-tuple-element.216, f32[1024]{0:T(1024)S(1)} %bitcast.134, f32[1024]{0:T(1024)S(1)} %bitcast.135, f32[1024]{0:T(1024)S(1)} %bitcast.136, f32[512,1024]{1,0:T(8,128)S(1)} %get-tuple-element.220, ...), kind=kLoop, calls=%fused_computation.18.clone.1 | loop fusion | flops 21494272 | bytes 8423424 | tf_op jit(solution)/shard_map/while/body/eval_jaxpr/while/body/eval_jaxpr/reduce_sum | solution.py:68
  (104 shorter events, 52.9 us)
Async XLA Ops:
  4.5 22.3 %collective-permute-start.1 = (f32[4,4,128]{2,0,1:T(4,128)S(1)}, f32[4,4,128]{2,0,1:T(4,128)S(1)}, u32[]{:S(2)}, u32[]{:S(2)}) collective-permute-start(f32[4,4,128]{2,0,1:T(4,128)S(1)} %get-tuple-element.151), channel_id=1, source_target_pairs={{1,0},{2,1},{3,2},{4,3},{5,4},{6,5},{7,6},{9,8},{10,9},{11,10},{12... | collective-permute-start | bytes 24584 | tf_op jit(solution)/shard_map/ppermute | solution.py:26
  6.8 20.1 %collective-permute-start = (f32[4,4,128]{2,0,1:T(4,128)S(1)}, f32[4,4,128]{2,0,1:T(4,128)S(1)}, u32[]{:S(2)}, u32[]{:S(2)}) collective-permute-start(f32[4,4,128]{2,0,1:T(4,128)S(1)} %get-tuple-element.150), channel_id=1, source_target_pairs={{0,1},{1,2},{2,3},{3,4},{4,5},{5,6},{6,7},{8,9},{9,10},{10,11},{11... | collective-permute-start | bytes 24584 | tf_op jit(solution)/shard_map/ppermute | solution.py:24
  14.3 12.6 %copy-start = (f32[3,512]{1,0:T(4,128)S(1)}, f32[3,512]{1,0:T(4,128)}, u32[]{:S(2)}) copy-start(f32[3,512]{1,0:T(4,128)} %param.13) | copy-start | bytes 18436
  14.3 12.6 %copy-start.2 = (f32[512]{0:T(512)S(1)}, f32[512]{0:T(512)}, u32[]{:S(2)}) copy-start(f32[512]{0:T(512)} %param.14) | copy-start | bytes 6148
  18.2 24.9 %collective-permute-start.2 = (f32[10,1024]{0,1:T(8,128)S(1)}, f32[10,1024]{0,1:T(8,128)S(1)}, u32[]{:S(2)}, u32[]{:S(2)}) collective-permute-start(f32[10,1024]{0,1:T(8,128)S(1)} %multiply_bitcast_fusion.4), channel_id=1, source_target_pairs={{0,512},{1,513},{2,514},{3,515},{4,516},{5,517},{6,518},{7,519},{8... | collective-permute-start | bytes 122888 | tf_op jit(solution)/shard_map/ppermute | solution.py:36
  47.3 12.2 %copy-start.1 = (f32[10,7168]{1,0:T(8,128)S(1)}, f32[10,7168]{1,0:T(8,128)}, u32[]{:S(2)}) copy-start(f32[10,7168]{1,0:T(8,128)} %get-tuple-element.134) | copy-start | bytes 860164
  48.7 32.4 %collective-permute-start.3 = (f32[10,1024]{0,1:T(8,128)S(1)}, f32[10,1024]{0,1:T(8,128)S(1)}, u32[]{:S(2)}, u32[]{:S(2)}) collective-permute-start(f32[10,1024]{0,1:T(8,128)S(1)} %multiply_bitcast_fusion.3), channel_id=1, source_target_pairs={{0,256},{1,257},{2,258},{3,259},{4,260},{5,261},{6,262},{7,263},{8... | collective-permute-start | bytes 122888 | tf_op jit(solution)/shard_map/ppermute | solution.py:36
  88.2 16.0 %collective-permute-start.4 = (f32[10,1024]{0,1:T(8,128)}, f32[10,1024]{0,1:T(8,128)S(1)}, u32[]{:S(2)}, u32[]{:S(2)}) collective-permute-start(f32[10,1024]{0,1:T(8,128)} %multiply_bitcast_fusion.2), channel_id=1, source_target_pairs={{0,128},{1,129},{2,130},{3,131},{4,132},{5,133},{6,134},{7,135},{8... | collective-permute-start | bytes 122888 | tf_op jit(solution)/shard_map/ppermute | solution.py:36
  110.8 26.0 %collective-permute-start.5 = (f32[10,1024]{0,1:T(8,128)S(1)}, f32[10,1024]{0,1:T(8,128)S(1)}, u32[]{:S(2)}, u32[]{:S(2)}) collective-permute-start(f32[10,1024]{0,1:T(8,128)S(1)} %multiply_bitcast_fusion.1), channel_id=1, source_target_pairs={{0,64},{1,65},{2,66},{3,67},{4,68},{5,69},{6,70},{7,71},{8,72},{9,... | collective-permute-start | bytes 122888 | tf_op jit(solution)/shard_map/ppermute | solution.py:36
  142.6 38.7 %collective-permute-start.6 = (f32[10,1024]{0,1:T(8,128)S(1)}, f32[10,1024]{0,1:T(8,128)S(1)}, u32[]{:S(2)}, u32[]{:S(2)}) collective-permute-start(f32[10,1024]{0,1:T(8,128)S(1)} %multiply_bitcast_fusion), channel_id=1, source_target_pairs={{0,32},{1,33},{2,34},{3,35},{4,36},{5,37},{6,38},{7,39},{8,40},{9,... | collective-permute-start | bytes 122888 | tf_op jit(solution)/shard_map/ppermute | solution.py:36
where the time goes:
time: 247 us; the launch traced here: 246 us
  waiting for transfers between devices  81.2 us (33%)
  other arithmetic  78.4 us (32%)
  starting transfers between devices  56 us (23%)
  local copies, waits for them, and re-layouts  29.7 us (12%)
    ppermute x5, waiting for transfers between devices, swapped(): return lax.ppermute(value, axis, pairs)  81.2 us
    ppermute x5, starting transfers between devices, swapped(): return lax.ppermute(value, axis, pairs)  49 us
    reduce_sum x7, other arithmetic, tile_accel(): jnp.sum(radial * offset[0] + quad_x * inverse_five, axis=1)  37.5 us
    sub x7, other arithmetic, tile_accel(): offset = targets[:, :, None] - sources[1:4, None, :]  25.3 us
    gather x5, local copies, waits for them, and re-layouts, shards(): jnp.take(held_cells, slot_index, axis=1)  20.5 us
  transfers between devices with their start and end apart: 7, of which 5 were waited for; matrix products, arithmetic and copies ran while one was open for 6% of the time, Pallas kernels for 0%

commit v1 on v0

v1 whole, which is shorter than its diff:
```python
import functools

import jax
import jax.numpy as jnp
from jax import lax
from jax.experimental import pallas as pl
from jax.experimental.pallas import tpu as pltpu
from jax.sharding import PartitionSpec as P

MESH = pl.DeviceIdType.MESH
AXES = ("gx", "gy", "gz")
SOFTEN = 0.01
LANES = 128
OWN = 2048 // LANES
SLOTS = 1024 // LANES
LIVE = 768 // LANES
GROUP = 32
KEEP = 8192


def row8(row):
    return jnp.broadcast_to(row, (8, LANES))


def flipped(value, bit):
    unit = 2**bit
    return value + unit - 2 * unit * lax.rem(lax.div(value, unit), 2)


def kernel(
    sizes,
    levels,
    pos_h,
    mass_h,
    cm_h,
    cc_h,
    cq_h,
    lists_h,
    masks_h,
    face_lists,
    face_counts,
    out_ref,
    pos,
    mass,
    cm,
    cc,
    cq,
    lists,
    masks,
    xb,
    acc,
    slot_ids,
    ranks,
    their_ranks,
    part,
    sent,
    got,
    bodies_out,
    bodies_in,
    in_sem,
    send_sem,
    recv_sem,
    rank_send_sem,
    rank_recv_sem,
    body_send_sem,
    body_recv_sem,
):
    nx, ny, nz = sizes
    bz, by = nz.bit_length() - 1, ny.bit_length() - 1
    bits = nx.bit_length() - 1 + by + bz
    gx, gy, gz = (lax.axis_index(a) for a in AXES)

    loads = {}
    for n, (name, src, dst) in enumerate(
        (
            ("lists", lists_h, lists),
            ("masks", masks_h, masks),
            ("cm", cm_h, cm),
            ("cc", cc_h, cc),
            ("cq", cq_h, cq),
            ("pos", pos_h, pos),
            ("mass", mass_h, mass),
        )
    ):
        loads[name] = pltpu.make_async_copy(src, dst, in_sem.at[n])
        loads[name].start()

    partners = []
    for level in range(levels):
        bit = bits - 1 - level
        if bit >= by + bz:
            partners.append((flipped(gx, bit - by - bz), gy, gz))
        elif bit >= bz:
            partners.append((gx, flipped(gy, bit - bz), gz))
        else:
            partners.append((gx, gy, flipped(gz, bit)))
    lower = (gx, gy, lax.rem(gz + nz - 1, nz))
    upper = (gx, gy, lax.rem(gz + 1, nz))
    barrier = pltpu.get_barrier_semaphore()
    for peer in partners + [lower, upper]:
        pl.semaphore_signal(barrier, inc=1, device_id=peer, device_id_type=MESH)

    loads["lists"].wait()
    loads["masks"].wait()
    lane = lax.broadcasted_iota(jnp.int32, (8, LANES), 1)

    def chunk8(ref, q):
        rows = ref[0, :, q * LANES : (q + 1) * LANES]
        pad = jnp.zeros((8 - levels, LANES), jnp.int32)
        return jnp.concatenate([rows, pad], axis=0) if levels < 8 else rows

    live = [chunk8(masks, q) for q in range(SLOTS)]
    stacked = jnp.concatenate(live, axis=0).astype(jnp.float32)
    earlier = (
        lax.broadcasted_iota(jnp.int32, (LANES, LANES), 0)
        < lax.broadcasted_iota(jnp.int32, (LANES, LANES), 1)
    ).astype(jnp.float32)
    before = jnp.dot(stacked, earlier, preferred_element_type=jnp.float32)
    totals = jnp.dot(
        stacked, jnp.ones((LANES, LANES), jnp.float32), preferred_element_type=jnp.float32
    )
    base = jnp.zeros((8, LANES), jnp.float32)
    packed = []
    for q in range(SLOTS):
        rank = (before[8 * q : 8 * q + 8] + base).astype(jnp.int32)
        base = base + totals[8 * q : 8 * q + 8]
        on = live[q] > 0
        where = jnp.where(on, rank, -1)
        for level in range(levels - 1):
            ranks[level, q : q + 1, :] = where[level : level + 1]
        moves = lane + q * LANES - rank
        packed.append(jnp.where(on, chunk8(lists, q) + moves * KEEP, 0))
    shift = 1
    while shift <= (SLOTS - LIVE) * LANES:
        flag = shift * KEEP
        if shift < LANES:
            turned = [pltpu.roll(w, LANES - shift, 1) for w in packed] + [jnp.zeros((8, LANES), jnp.int32)]
            coming = [
                jnp.where(lane < LANES - shift, turned[q], turned[q + 1]) for q in range(SLOTS)
            ]
        else:
            step = shift // LANES
            coming = [
                packed[q + step] if q + step < SLOTS else jnp.zeros((8, LANES), jnp.int32)
                for q in range(SLOTS)
            ]
        packed = [
            jnp.where((c & flag) != 0, c, jnp.where((w & flag) != 0, 0, w))
            for c, w in zip(coming, packed)
        ]
        shift *= 2
    for q in range(LIVE):
        slots = packed[q] & (KEEP - 1)
        for level in range(levels):
            slot_ids[level, q : q + 1, :] = slots[level : level + 1]
    for level in range(levels):
        slot_ids[level, LIVE:, :] = jnp.full((8 - LIVE, LANES), -1, jnp.int32)

    def own_row(c, k):
        if c == 0:
            return cm[pl.ds(k, 1), :]
        ref, r = (cc, c - 1) if c < 4 else (cq, c - 4)
        if isinstance(k, int):
            return ref[r : r + 1, k * LANES : (k + 1) * LANES]
        return ref[r : r + 1, pl.ds(pl.multiple_of(k * LANES, LANES), LANES)]

    def got_row(level):
        return lambda c, k: got[level, c * LIVE + k : c * LIVE + k + 1, :]

    def pick_own(level):
        ids = slot_ids[level]
        rows, cols = ids >> 7, ids & (LANES - 1)

        def step(k, found):
            here = rows == k
            return tuple(
                jnp.where(here, jnp.take_along_axis(row8(own_row(c, k)), cols, axis=1), found[c])
                for c in range(10)
            )

        found = tuple(jnp.zeros((8, LANES), jnp.float32) for _ in range(10))
        found = lax.fori_loop(0, OWN, step, found, unroll=8)
        return list(found)

    def pick_got(level, source, found):
        ids = slot_ids[level]
        rows, cols = ids >> 7, ids & (LANES - 1)
        for k in range(LIVE):
            here = rows == OWN + source * SLOTS + k
            for c in range(10):
                row = row8(got_row(source)(c, k))
                found[c] = jnp.where(here, jnp.take_along_axis(row, cols, axis=1), found[c])
        return found

    def translate(level, source):
        ids = slot_ids[level]
        rows, cols = ids >> 7, ids & (LANES - 1)
        first = OWN + source * SLOTS
        place = ids
        for k in range(SLOTS):
            row = row8(their_ranks[source, k : k + 1, :])
            value = jnp.take_along_axis(row, cols, axis=1)
            value = jnp.where(value < 0, -1, value + first * LANES)
            place = jnp.where(rows == first + k, value, place)
        slot_ids[level] = place

    def send(level, found):
        for c in range(10):
            sent[level, c * LIVE : (c + 1) * LIVE, :] = found[c][:LIVE]
        copies[level].start()

    copies = [
        pltpu.make_async_remote_copy(
            src_ref=sent.at[level],
            dst_ref=got.at[level],
            send_sem=send_sem.at[level],
            recv_sem=recv_sem.at[level],
            device_id=partners[level],
            device_id_type=MESH,
        )
        for level in range(levels)
    ]
    rank_copies = [
        pltpu.make_async_remote_copy(
            src_ref=ranks.at[level],
            dst_ref=their_ranks.at[level],
            send_sem=rank_send_sem.at[level],
            recv_sem=rank_recv_sem.at[level],
            device_id=partners[level],
            device_id_type=MESH,
        )
        for level in range(levels - 1)
    ]
    body_copies = [
        pltpu.make_async_remote_copy(
            src_ref=bodies_out.at[side],
            dst_ref=bodies_in.at[1 - side],
            send_sem=body_send_sem.at[side],
            recv_sem=body_recv_sem.at[1 - side],
            device_id=peer,
            device_id_type=MESH,
        )
        for side, peer in enumerate((lower, upper))
    ]

    loads["cm"].wait()
    loads["cc"].wait()
    loads["cq"].wait()
    found = pick_own(0)
    for c in range(10):
        sent[0, c * LIVE : (c + 1) * LIVE, :] = found[c][:LIVE]
    loads["pos"].wait()
    loads["mass"].wait()
    for side in range(2):
        for block in range(4):
            listed = jnp.int32(0)
            for j in range(4):
                hit = (face_lists[0, side, j] == block) & (j < face_counts[0, side])
                listed = listed + hit.astype(jnp.int32)
            kept = jnp.where(listed > 0, mass[block : block + 1, :], 0.0)
            bodies_out[side, block : block + 1, :] = kept
        for a in range(3):
            for block in range(4):
                bodies_out[side, 4 + 4 * a + block : 5 + 4 * a + block, :] = pos[
                    a : a + 1, block * LANES : (block + 1) * LANES
                ]

    pl.semaphore_wait(barrier, levels + 2)
    copies[0].start()
    for copy in rank_copies + body_copies:
        copy.start()

    for a in range(3):
        for block in range(4):
            row = pos[a : a + 1, block * LANES : (block + 1) * LANES]
            xb[a, block * LANES : (block + 1) * LANES, :] = jnp.broadcast_to(
                row, (LANES, LANES)
            ).T
    acc[...] = jnp.zeros_like(acc)

    def add_cells(read, rows, first, count):
        def step(g, _):
            at = pl.multiple_of(first + g * GROUP, GROUP)
            x = [xb[a, pl.ds(at, GROUP), :] for a in range(3)]
            total = [acc[a, pl.ds(at, GROUP), :] for a in range(3)]
            for k in rows:
                m, c0, c1, c2, xx, yy, zz, xy, xz, yz = (read(c, k) for c in range(10))
                d0, d1, d2 = x[0] - c0, x[1] - c1, x[2] - c2
                s = (d0 * d0 + d1 * d1) + (d2 * d2 + SOFTEN)
                u = lax.rsqrt(s)
                u2 = u * u
                q0 = xx * d0 + xy * d1 + xz * d2
                q1 = xy * d0 + yy * d1 + yz * d2
                q2 = xz * d0 + yz * d1 + zz * d2
                form = d0 * q0 + d1 * q1 + d2 * q2
                u5 = u2 * u2 * u
                w = m * s + 2.5 * (form * u2)
                total[0] = total[0] + u5 * (q0 - w * d0)
                total[1] = total[1] + u5 * (q1 - w * d1)
                total[2] = total[2] + u5 * (q2 - w * d2)
            for a in range(3):
                acc[a, pl.ds(at, GROUP), :] = total[a]
            return 0

        lax.fori_loop(0, count // GROUP, step, 0)

    def add_bodies(read, rows):
        def step(g, _):
            at = pl.multiple_of(g * GROUP, GROUP)
            x = [xb[a, pl.ds(at, GROUP), :] for a in range(3)]
            total = [acc[a, pl.ds(at, GROUP), :] for a in range(3)]
            for k in rows:
                m, c0, c1, c2 = (read(c, k) for c in range(4))
                d0, d1, d2 = x[0] - c0, x[1] - c1, x[2] - c2
                s = (d0 * d0 + d1 * d1) + (d2 * d2 + SOFTEN)
                u = lax.rsqrt(s)
                p = m * (u * u * u)
                total[0] = total[0] - p * d0
                total[1] = total[1] - p * d1
                total[2] = total[2] - p * d2
            for a in range(3):
                acc[a, pl.ds(at, GROUP), :] = total[a]
            return 0

        lax.fori_loop(0, 512 // GROUP, step, 0)

    def own(lo, hi):
        add_cells(own_row, range(lo, hi), 0, 512)

    def arrived(level):
        add_cells(got_row(level), range(LIVE), 0, 512)

    def own_bodies(c, k):
        if c == 0:
            return mass[k : k + 1, :]
        return pos[c - 1 : c, k * LANES : (k + 1) * LANES]

    def near(side):
        body_copies[1 - side].wait_recv()
        inside = (gz > 0) if side == 0 else (gz < nz - 1)

        @pl.when(inside)
        def _():
            add_bodies(lambda c, k: bodies_in[side, 4 * c + k : 4 * c + k + 1, :], range(4))

    def keep(level, found):
        for c in range(10):
            part[level, c] = found[c]

    def kept(level):
        return [part[level, c] for c in range(10)]

    for level in range(1, levels):
        keep(level, pick_own(level))
    work = [
        [lambda: own(0, 6), lambda: own(6, 12)],
        [lambda: add_bodies(own_bodies, range(4)), lambda: own(12, 16)],
        [lambda: near(0), lambda: near(1), lambda: arrived(0)],
        [lambda: arrived(1), lambda: arrived(2)],
        [lambda: arrived(3)],
    ]
    for level in range(levels):
        for job in work[level]:
            job()
        if level < levels - 1:
            rank_copies[level].wait_recv()
            for later in range(level + 1, levels):
                translate(later, level)
            copies[level].wait_recv()
            send(level + 1, pick_got(level + 1, level, kept(level + 1)))
            for later in range(level + 2, levels):
                keep(later, pick_got(later, level, kept(later)))
        else:
            copies[level].wait_recv()
    for block in range(4):
        add_cells(got_row(levels - 1), range(LIVE), block * LANES, LANES)
        for a in range(3):
            turned = acc[a, block * LANES : (block + 1) * LANES, :].T
            out_ref[a : a + 1, block * LANES : (block + 1) * LANES] = jnp.sum(
                turned, axis=0, keepdims=True
            )
    for copy in copies + rank_copies + body_copies:
        copy.wait_send()


def shards(sizes, pos, mass, cm, cc, cq, lists, masks, face_lists, face_counts):
    levels = lists.shape[1]
    f32, i32 = jnp.float32, jnp.int32
    any_space = pl.BlockSpec(memory_space=pl.ANY)
    smem = pl.BlockSpec(memory_space=pltpu.SMEM)
    dma = pltpu.SemaphoreType.DMA
    return pl.pallas_call(
        functools.partial(kernel, sizes, levels),
        out_shape=jax.ShapeDtypeStruct(pos.shape, f32),
        in_specs=[any_space] * 7 + [smem] * 2,
        out_specs=pl.BlockSpec(memory_space=pltpu.VMEM),
        scratch_shapes=[
            pltpu.VMEM(pos.shape, f32),
            pltpu.VMEM((4, LANES), f32),
            pltpu.VMEM((OWN, LANES), f32),
            pltpu.VMEM(cc.shape, f32),
            pltpu.VMEM(cq.shape, f32),
            pltpu.VMEM(lists.shape, i32),
            pltpu.VMEM(masks.shape, i32),
            pltpu.VMEM((3, 512, LANES), f32),
            pltpu.VMEM((3, 512, LANES), f32),
            pltpu.VMEM((levels, 8, LANES), i32),
            pltpu.VMEM((levels - 1, SLOTS, LANES), i32),
            pltpu.VMEM((levels - 1, SLOTS, LANES), i32),
            pltpu.VMEM((levels, 10, 8, LANES), f32),
            pltpu.VMEM((levels, 10 * LIVE, LANES), f32),
            pltpu.VMEM((levels, 10 * LIVE, LANES), f32),
            pltpu.VMEM((2, 16, LANES), f32),
            pltpu.VMEM((2, 16, LANES), f32),
            dma((7,)),
            dma((levels,)),
            dma((levels,)),
            dma((levels - 1,)),
            dma((levels - 1,)),
            dma((2,)),
            dma((2,)),
        ],
        compiler_params=pltpu.CompilerParams(collective_id=0, has_side_effects=True),
        name="treecode",
    )(
        pos,
        mass.reshape(4, LANES),
        cm.reshape(OWN, LANES),
        cc,
        cq,
        lists,
        masks,
        face_lists,
        face_counts,
    )


def solution(mesh):
    sizes = tuple(mesh.shape[a] for a in AXES)
    in_specs = (
        P(None, AXES),
        P(AXES),
        P(AXES),
        P(None, AXES),
        P(None, AXES),
        P(AXES, None, None),
        P(AXES, None, None),
        P(AXES, None, None),
        P(AXES, None),
    )
    return jax.shard_map(
        functools.partial(shards, sizes),
        mesh=mesh,
        in_specs=in_specs,
        out_specs=P(None, AXES),
        check_vma=False,
    )
```

time: 247 us -> 50.5 us (0.20)
  the two profiles are of different devices: /device:TPU:48 before, /device:TPU:96 now
where the time goes in v1:
time: 50.5 us; the launch traced here: 50.2 us
  Pallas kernels  46.9 us (93%)
  local copies, waits for them, and re-layouts  3.28 us (6%)
    pallas_call x1, Pallas kernels, shards(): pl.pallas_call(functools.partial(kernel, sizes, levels), out_shape=jax.Sh...  46.9 us
    unnamed x5, local copies, waits for them, and re-layouts  3.28 us

profile of v1, /device:TPU:96, one launch (start us, length us, event | category | flops | bytes accessed | tf_op | source)
XLA Modules:
  0.0 50.2 jit_solution(7003949314199647812)
XLA Ops:
  0.0 0.0 copy-start
  0.0 1.4 %copy.10.lists_h = s32[1,5,1024]{2,1,0:T(8,128)} copy(s32[1,5,1024]{2,0,1:T(1,128)} %param.14) | data formatting | bytes 40960 | tf_op args[5]
  1.4 0.0 copy-done
  1.4 0.6 %copy.11.masks_h = s32[1,5,1024]{2,1,0:T(8,128)} copy(s32[1,5,1024]{2,0,1:T(1,128)S(1)} %copy-done) | data formatting | bytes 40960 | tf_op args[6]
  2.0 46.9 %treecode.1 = f32[3,512]{1,0:T(4,128)} custom-call(f32[3,512]{1,0:T(4,128)} %pos_h.1, f32[4,128]{1,0:T(4,128)} %bitcast.3, f32[16,128]{1,0:T(8,128)} %bitcast.2, f32[3,2048]{1,0:T(4,128)} %cc_h.1, f32[6,2048]{1,0:T(8,128)} %cq_h.1, s32[1,5,1024]{2,1,0:T(8,128)} %copy.10.lists_h, s32[1,5,1024]{2,1,0:T(8,128)} %copy.11.masks_h, s32[1,2,4]{2,1,0:T(2,128)} %face_lists.1, ...), custom_call_target="tpu_custom_call" | custom-call | tf_op jit(solution)/shard_map/treecode/pallas_call | solution.py:392
  48.9 1.3 %copy.13 = f32[3,512]{1,0:T(4,128)} copy(f32[3,512]{1,0:T(4,128)} %treecode.1) | data formatting | bytes 12288
Async XLA Ops:
  0.0 1.4 %copy-start = (s32[1,5,1024]{2,0,1:T(1,128)S(1)}, s32[1,5,1024]{2,0,1:T(1,128)}, u32[]{:S(2)}) copy-start(s32[1,5,1024]{2,0,1:T(1,128)} %param.15) | copy-start | bytes 61444

commit v2 on v1

--- a/solution.py
+++ b/solution.py
@@ -14,8 +14,18 @@
 OWN = 2048 // LANES
 SLOTS = 1024 // LANES
 LIVE = 768 // LANES
+COMPS = 10
+BLOCK = 64
 GROUP = 32
 KEEP = 8192
+PLAN = (
+    (8, 7, 2, 0),
+    (8, 8, 3, 1),
+    (9, 10, 5, 3),
+    (11, 11, 7, 5),
+    (15, 13, 9, 7),
+    (20, 20, 12, 10),
+)
 
 
 def row8(row):
@@ -54,7 +64,7 @@
     their_ranks,
     part,
     sent,
-    got,
+    table,
     bodies_out,
     bodies_in,
     in_sem,
@@ -100,72 +110,66 @@
     for peer in partners + [lower, upper]:
         pl.semaphore_signal(barrier, inc=1, device_id=peer, device_id_type=MESH)
 
+    late = lax.rem(gx, 2) * 2 + lax.div(gy, 4)
+    others = lax.div((gx * ny + gy) * nz + gz + nx * ny * nz - 1, nx * ny * nz)
+    late = late + 3 * (1 - others)
+    steps = [lax.div(late + 3, 4), lax.div(late + 2, 4), lax.div(late + 1, 4)]
+
+    def bound(window):
+        b = PLAN[window]
+        return b[0] + sum((b[i + 1] - b[i]) * steps[i] for i in range(3))
+
     loads["lists"].wait()
     loads["masks"].wait()
     lane = lax.broadcasted_iota(jnp.int32, (8, LANES), 1)
-
-    def chunk8(ref, q):
-        rows = ref[0, :, q * LANES : (q + 1) * LANES]
-        pad = jnp.zeros((8 - levels, LANES), jnp.int32)
-        return jnp.concatenate([rows, pad], axis=0) if levels < 8 else rows
-
-    live = [chunk8(masks, q) for q in range(SLOTS)]
-    stacked = jnp.concatenate(live, axis=0).astype(jnp.float32)
-    earlier = (
-        lax.broadcasted_iota(jnp.int32, (LANES, LANES), 0)
-        < lax.broadcasted_iota(jnp.int32, (LANES, LANES), 1)
-    ).astype(jnp.float32)
-    before = jnp.dot(stacked, earlier, preferred_element_type=jnp.float32)
-    totals = jnp.dot(
-        stacked, jnp.ones((LANES, LANES), jnp.float32), preferred_element_type=jnp.float32
-    )
-    base = jnp.zeros((8, LANES), jnp.float32)
+    slot = lax.broadcasted_iota(jnp.int32, (8, LANES), 0) * LANES + lane
+
+    def dot(x, y):
+        return jnp.dot(x, y, preferred_element_type=jnp.float32)
+
+    def square(n, test):
+        i = lax.broadcasted_iota(jnp.int32, (n, n), 0)
+        j = lax.broadcasted_iota(jnp.int32, (n, n), 1)
+        return test(i, j).astype(jnp.float32)
+
+    stacked = jnp.concatenate([masks[level] for level in range(levels)], axis=0)
+    stacked = stacked.astype(jnp.float32)
+    before = dot(stacked, square(LANES, lambda i, j: i < j))
+    totals = dot(stacked, jnp.ones((LANES, LANES), jnp.float32))
+    base = dot(square(8 * levels, lambda i, j: ((i >> 3) == (j >> 3)) & (i > j)), totals)
+    rank = (before + base).astype(jnp.int32)
     packed = []
-    for q in range(SLOTS):
-        rank = (before[8 * q : 8 * q + 8] + base).astype(jnp.int32)
-        base = base + totals[8 * q : 8 * q + 8]
-        on = live[q] > 0
-        where = jnp.where(on, rank, -1)
-        for level in range(levels - 1):
-            ranks[level, q : q + 1, :] = where[level : level + 1]
-        moves = lane + q * LANES - rank
-        packed.append(jnp.where(on, chunk8(lists, q) + moves * KEEP, 0))
+    for level in range(levels):
+        place = rank[8 * level : 8 * level + 8]
+        on = masks[level] > 0
+        if level < levels - 1:
+            ranks[level] = jnp.where(on, place, -1)
+        packed.append(jnp.where(on, lists[level] + (slot - place) * KEEP, 0))
     shift = 1
     while shift <= (SLOTS - LIVE) * LANES:
         flag = shift * KEEP
-        if shift < LANES:
-            turned = [pltpu.roll(w, LANES - shift, 1) for w in packed] + [jnp.zeros((8, LANES), jnp.int32)]
-            coming = [
-                jnp.where(lane < LANES - shift, turned[q], turned[q + 1]) for q in range(SLOTS)
-            ]
-        else:
-            step = shift // LANES
-            coming = [
-                packed[q + step] if q + step < SLOTS else jnp.zeros((8, LANES), jnp.int32)
-                for q in range(SLOTS)
-            ]
-        packed = [
-            jnp.where((c & flag) != 0, c, jnp.where((w & flag) != 0, 0, w))
-            for c, w in zip(coming, packed)
-        ]
+        for level in range(levels):
+            w = packed[level]
+            if shift < LANES:
+                turned = pltpu.roll(w, LANES - shift, 1)
+                coming = jnp.where(lane < LANES - shift, turned, pltpu.roll(turned, 7, 0))
+            else:
+                coming = pltpu.roll(w, 8 - shift // LANES, 0)
+            coming = jnp.where(slot < SLOTS * LANES - shift, coming, 0)
+            stay = jnp.where((w & flag) != 0, 0, w)
+            packed[level] = jnp.where((coming & flag) != 0, coming, stay)
         shift *= 2
-    for q in range(LIVE):
-        slots = packed[q] & (KEEP - 1)
-        for level in range(levels):
-            slot_ids[level, q : q + 1, :] = slots[level : level + 1]
     for level in range(levels):
-        slot_ids[level, LIVE:, :] = jnp.full((8 - LIVE, LANES), -1, jnp.int32)
+        slot_ids[level] = jnp.where(slot < LIVE * LANES, packed[level] & (KEEP - 1), -1)
+
+    def level_start(level):
+        return OWN * COMPS + BLOCK * level
 
     def own_row(c, k):
-        if c == 0:
-            return cm[pl.ds(k, 1), :]
-        ref, r = (cc, c - 1) if c < 4 else (cq, c - 4)
-        if isinstance(k, int):
-            return ref[r : r + 1, k * LANES : (k + 1) * LANES]
-        return ref[r : r + 1, pl.ds(pl.multiple_of(k * LANES, LANES), LANES)]
+        return table[pl.ds(k * COMPS + c, 1), :]
 
     def got_row(level):
-        return lambda c, k: got[level, c * LIVE + k : c * LIVE + k + 1, :]
+        return lambda c, k: table[pl.ds(level_start(level) + k * COMPS + c, 1), :]
 
     def pick_own(level):
         ids = slot_ids[level]
@@ -204,15 +208,18 @@
             place = jnp.where(rows == first + k, value, place)
         slot_ids[level] = place
 
+    def stage(level, found):
+        for c in range(COMPS):
+            sent[level, pl.ds(c, LIVE, stride=COMPS), :] = found[c][:LIVE]
+
     def send(level, found):
-        for c in range(10):
-            sent[level, c * LIVE : (c + 1) * LIVE, :] = found[c][:LIVE]
+        stage(level, found)
         copies[level].start()
 
     copies = [
         pltpu.make_async_remote_copy(
             src_ref=sent.at[level],
-            dst_ref=got.at[level],
+            dst_ref=table.at[pl.ds(level_start(level), BLOCK)],
             send_sem=send_sem.at[level],
             recv_sem=recv_sem.at[level],
             device_id=partners[level],
@@ -246,9 +253,12 @@
     loads["cm"].wait()
     loads["cc"].wait()
     loads["cq"].wait()
-    found = pick_own(0)
-    for c in range(10):
-        sent[0, c * LIVE : (c + 1) * LIVE, :] = found[c][:LIVE]
+    for k in range(OWN):
+        cols = slice(k * LANES, (k + 1) * LANES)
+        table[k * COMPS : k * COMPS + 1, :] = cm[k : k + 1, :]
+        table[k * COMPS + 1 : k * COMPS + 4, :] = cc[:, cols]
+        table[k * COMPS + 4 : (k + 1) * COMPS, :] = cq[:, cols]
+    stage(0, pick_own(0))
     loads["pos"].wait()
     loads["mass"].wait()
     for side in range(2):
@@ -257,52 +267,60 @@
             for j in range(4):
                 hit = (face_lists[0, side, j] == block) & (j < face_counts[0, side])
                 listed = listed + hit.astype(jnp.int32)
-            kept = jnp.where(listed > 0, mass[block : block + 1, :], 0.0)
-            bodies_out[side, block : block + 1, :] = kept
+            kept_mass = jnp.where(listed > 0, mass[block : block + 1, :], 0.0)
+            bodies_out[side, block : block + 1, :] = kept_mass
         for a in range(3):
             for block in range(4):
                 bodies_out[side, 4 + 4 * a + block : 5 + 4 * a + block, :] = pos[
                     a : a + 1, block * LANES : (block + 1) * LANES
                 ]
 
-    pl.semaphore_wait(barrier, levels + 2)
-    copies[0].start()
-    for copy in rank_copies + body_copies:
-        copy.start()
-
-    for a in range(3):
-        for block in range(4):
-            row = pos[a : a + 1, block * LANES : (block + 1) * LANES]
-            xb[a, block * LANES : (block + 1) * LANES, :] = jnp.broadcast_to(
-                row, (LANES, LANES)
-            ).T
-    acc[...] = jnp.zeros_like(acc)
-
-    def add_cells(read, rows, first, count):
-        def step(g, _):
-            at = pl.multiple_of(first + g * GROUP, GROUP)
-            x = [xb[a, pl.ds(at, GROUP), :] for a in range(3)]
-            total = [acc[a, pl.ds(at, GROUP), :] for a in range(3)]
-            for k in rows:
-                m, c0, c1, c2, xx, yy, zz, xy, xz, yz = (read(c, k) for c in range(10))
-                d0, d1, d2 = x[0] - c0, x[1] - c1, x[2] - c2
-                s = (d0 * d0 + d1 * d1) + (d2 * d2 + SOFTEN)
-                u = lax.rsqrt(s)
-                u2 = u * u
-                q0 = xx * d0 + xy * d1 + xz * d2
-                q1 = xy * d0 + yy * d1 + yz * d2
-                q2 = xz * d0 + yz * d1 + zz * d2
-                form = d0 * q0 + d1 * q1 + d2 * q2
-                u5 = u2 * u2 * u
-                w = m * s + 2.5 * (form * u2)
-                total[0] = total[0] + u5 * (q0 - w * d0)
-                total[1] = total[1] + u5 * (q1 - w * d1)
-                total[2] = total[2] + u5 * (q2 - w * d2)
-            for a in range(3):
-                acc[a, pl.ds(at, GROUP), :] = total[a]
-            return 0
-
-        lax.fori_loop(0, count // GROUP, step, 0)
+    def spread():
+        for a in range(3):
+            for block in range(4):
+                row = pos[a : a + 1, block * LANES : (block + 1) * LANES]
+                xb[a, block * LANES : (block + 1) * LANES, :] = jnp.broadcast_to(
+                    row, (LANES, LANES)
+                ).T
+        acc[...] = jnp.zeros_like(acc)
+
+    def cells_step(read, units, at):
+        x = [xb[a, pl.ds(at, GROUP), :] for a in range(3)]
+        total = [acc[a, pl.ds(at, GROUP), :] for a in range(3)]
+        for k in units:
+            m, c0, c1, c2, xx, yy, zz, xy, xz, yz = (read(c, k) for c in range(COMPS))
+            d0, d1, d2 = x[0] - c0, x[1] - c1, x[2] - c2
+            s = (d0 * d0 + d1 * d1) + (d2 * d2 + SOFTEN)
+            u = lax.rsqrt(s)
+            u2 = u * u
+            q0 = xx * d0 + xy * d1 + xz * d2
+            q1 = xy * d0 + yy * d1 + yz * d2
+            q2 = xz * d0 + yz * d1 + zz * d2
+            form = d0 * q0 + d1 * q1 + d2 * q2
+            u5 = u2 * u2 * u
+            w = m * s + 2.5 * (form * u2)
+            total[0] = total[0] + u5 * (q0 - w * d0)
+            total[1] = total[1] + u5 * (q1 - w * d1)
+            total[2] = total[2] + u5 * (q2 - w * d2)
+        for a in range(3):
+            acc[a, pl.ds(at, GROUP), :] = total[a]
+
+    def add_pairs(lo, hi):
+        def pair(p, _):
+            level = lax.div(jnp.maximum(p - 8, 0), 3)
+            start = 2 * COMPS * p + (BLOCK - LIVE * COMPS) * level
+
+            def step(g, _):
+                cells_step(
+                    lambda c, k: table[pl.ds(start + COMPS * k + c, 1), :],
+                    range(2),
+                    pl.multiple_of(g * GROUP, GROUP),
+                )
+                return 0
+
+            return lax.fori_loop(0, 512 // GROUP, step, 0)
+
+        lax.fori_loop(lo, hi, pair, 0)
 
     def add_bodies(read, rows):
         def step(g, _):
@@ -324,12 +342,6 @@
 
         lax.fori_loop(0, 512 // GROUP, step, 0)
 
-    def own(lo, hi):
-        add_cells(own_row, range(lo, hi), 0, 512)
-
-    def arrived(level):
-        add_cells(got_row(level), range(LIVE), 0, 512)
-
     def own_bodies(c, k):
         if c == 0:
             return mass[k : k + 1, :]
@@ -350,30 +362,43 @@
     def kept(level):
         return [part[level, c] for c in range(10)]
 
+    early = late < 3
+
+    @pl.when(early)
+    def _():
+        spread()
+        add_pairs(0, bound(0))
+
+    pl.semaphore_wait(barrier, levels + 2)
+    copies[0].start()
+    for copy in rank_copies + body_copies:
+        copy.start()
+
+    @pl.when(jnp.logical_not(early))
+    def _():
+        spread()
+
     for level in range(1, levels):
         keep(level, pick_own(level))
-    work = [
-        [lambda: own(0, 6), lambda: own(6, 12)],
-        [lambda: add_bodies(own_bodies, range(4)), lambda: own(12, 16)],
-        [lambda: near(0), lambda: near(1), lambda: arrived(0)],
-        [lambda: arrived(1), lambda: arrived(2)],
-        [lambda: arrived(3)],
-    ]
     for level in range(levels):
-        for job in work[level]:
-            job()
+        if level == 3:
+            add_bodies(own_bodies, range(4))
+            near(0)
+            near(1)
+        add_pairs(bound(level), bound(level + 1))
         if level < levels - 1:
             rank_copies[level].wait_recv()
             for later in range(level + 1, levels):
                 translate(later, level)
-            copies[level].wait_recv()
+        copies[level].wait_recv()
+        if level < levels - 1:
             send(level + 1, pick_got(level + 1, level, kept(level + 1)))
             for later in range(level + 2, levels):
                 keep(later, pick_got(later, level, kept(later)))
-        else:
-            copies[level].wait_recv()
+    add_pairs(bound(levels), 8 + 3 * (levels - 1))
     for block in range(4):
-        add_cells(got_row(levels - 1), range(LIVE), block * LANES, LANES)
+        for g in range(LANES // GROUP):
+            cells_step(got_row(levels - 1), range(LIVE), block * LANES + g * GROUP)
         for a in range(3):
             turned = acc[a, block * LANES : (block + 1) * LANES, :].T
             out_ref[a : a + 1, block * LANES : (block + 1) * LANES] = jnp.sum(
@@ -400,16 +425,16 @@
             pltpu.VMEM((OWN, LANES), f32),
             pltpu.VMEM(cc.shape, f32),
             pltpu.VMEM(cq.shape, f32),
-            pltpu.VMEM(lists.shape, i32),
-            pltpu.VMEM(masks.shape, i32),
+            pltpu.VMEM((levels, SLOTS, LANES), i32),
+            pltpu.VMEM((levels, SLOTS, LANES), i32),
             pltpu.VMEM((3, 512, LANES), f32),
             pltpu.VMEM((3, 512, LANES), f32),
             pltpu.VMEM((levels, 8, LANES), i32),
             pltpu.VMEM((levels - 1, SLOTS, LANES), i32),
             pltpu.VMEM((levels - 1, SLOTS, LANES), i32),
             pltpu.VMEM((levels, 10, 8, LANES), f32),
-            pltpu.VMEM((levels, 10 * LIVE, LANES), f32),
-            pltpu.VMEM((levels, 10 * LIVE, LANES), f32),
+            pltpu.VMEM((levels, BLOCK, LANES), f32),
+            pltpu.VMEM((OWN * COMPS + levels * BLOCK, LANES), f32),
             pltpu.VMEM((2, 16, LANES), f32),
             pltpu.VMEM((2, 16, LANES), f32),
             dma((7,)),
@@ -428,8 +453,8 @@
         cm.reshape(OWN, LANES),
         cc,
         cq,
-        lists,
-        masks,
+        lists.reshape(levels, SLOTS, LANES),
+        masks.reshape(levels, SLOTS, LANES),
         face_lists,
         face_counts,
     )

time: 50.5 us -> 45 us (0.89)
  the two profiles are of different devices: /device:TPU:96 before, /device:TPU:4 now
where the time goes in v2:
time: 45 us; the launch traced here: 44.8 us
  Pallas kernels  43.5 us (97%)
  local copies, waits for them, and re-layouts  1.3 us (3%)
    pallas_call x1, Pallas kernels, shards(): pl.pallas_call(functools.partial(kernel, sizes, levels), out_shape=jax.Sh...  43.5 us
    unnamed x1, local copies, waits for them, and re-layouts  1.3 us

profile of v2, /device:TPU:4, one launch (start us, length us, event | category | flops | bytes accessed | tf_op | source)
XLA Modules:
  0.0 44.8 jit_solution(4054036583545630565)
XLA Ops:
  0.0 43.5 %treecode.1 = f32[3,512]{1,0:T(4,128)} custom-call(f32[3,512]{1,0:T(4,128)} %pos_h.1, f32[4,128]{1,0:T(4,128)} %bitcast.7, f32[16,128]{1,0:T(8,128)} %bitcast.6, f32[3,2048]{1,0:T(4,128)} %cc_h.1, f32[6,2048]{1,0:T(8,128)} %cq_h.1, s32[5,8,128]{2,1,0:T(8,128)} %bitcast.4, s32[5,8,128]{2,1,0:T(8,128)} %bitcast.5, s32[1,2,4]{2,1,0:T(2,128)} %face_lists.1, ...), custom_call_target="tpu_custom_call" | custom-call | tf_op jit(solution)/shard_map/treecode/pallas_call | solution.py:417
  43.5 1.3 %copy.11 = f32[3,512]{1,0:T(4,128)} copy(f32[3,512]{1,0:T(4,128)} %treecode.1) | data formatting | bytes 12288

commit v3 on v2

--- a/solution.py
+++ b/solution.py
@@ -18,12 +18,13 @@
 BLOCK = 64
 GROUP = 32
 KEEP = 8192
+STEPS = ((0, 1), (2,), (3,), (4,))
+BODIES = 2
 PLAN = (
     (8, 7, 2, 0),
-    (8, 8, 3, 1),
-    (9, 10, 5, 3),
-    (11, 11, 7, 5),
-    (15, 13, 9, 7),
+    (8, 8, 4, 1),
+    (11, 10, 6, 3),
+    (15, 12, 8, 6),
     (20, 20, 12, 10),
 )
 
@@ -74,6 +75,12 @@
     rank_recv_sem,
     body_send_sem,
     body_recv_sem,
+    far_cells,
+    far_ranks,
+    near_ids,
+    ids_out,
+    far_send_sem,
+    far_recv_sem,
 ):
     nx, ny, nz = sizes
     bz, by = nz.bit_length() - 1, ny.bit_length() - 1
@@ -95,19 +102,21 @@
         loads[name] = pltpu.make_async_copy(src, dst, in_sem.at[n])
         loads[name].start()
 
-    partners = []
-    for level in range(levels):
+    def across(at, level):
         bit = bits - 1 - level
         if bit >= by + bz:
-            partners.append((flipped(gx, bit - by - bz), gy, gz))
-        elif bit >= bz:
-            partners.append((gx, flipped(gy, bit - bz), gz))
-        else:
-            partners.append((gx, gy, flipped(gz, bit)))
+            return (flipped(at[0], bit - by - bz), at[1], at[2])
+        if bit >= bz:
+            return (at[0], flipped(at[1], bit - bz), at[2])
+        return (at[0], at[1], flipped(at[2], bit))
+
+    partners = [across((gx, gy, gz), level) for level in range(levels)]
+    joined = [step for step in STEPS if len(step) == 2]
+    far_peers = [across(partners[step[0]], step[1]) for step in joined]
     lower = (gx, gy, lax.rem(gz + nz - 1, nz))
     upper = (gx, gy, lax.rem(gz + 1, nz))
     barrier = pltpu.get_barrier_semaphore()
-    for peer in partners + [lower, upper]:
+    for peer in partners + far_peers + [lower, upper]:
         pl.semaphore_signal(barrier, inc=1, device_id=peer, device_id_type=MESH)
 
     late = lax.rem(gx, 2) * 2 + lax.div(gy, 4)
@@ -161,6 +170,8 @@
         shift *= 2
     for level in range(levels):
         slot_ids[level] = jnp.where(slot < LIVE * LANES, packed[level] & (KEEP - 1), -1)
+    for n, step in enumerate(joined):
+        ids_out[n] = slot_ids[step[1]]
 
     def level_start(level):
         return OWN * COMPS + BLOCK * level
@@ -196,17 +207,35 @@
                 found[c] = jnp.where(here, jnp.take_along_axis(row, cols, axis=1), found[c])
         return found
 
-    def translate(level, source):
-        ids = slot_ids[level]
+    def placed(ids, source, table_of_ranks):
         rows, cols = ids >> 7, ids & (LANES - 1)
         first = OWN + source * SLOTS
         place = ids
         for k in range(SLOTS):
-            row = row8(their_ranks[source, k : k + 1, :])
+            row = row8(table_of_ranks[k : k + 1, :])
             value = jnp.take_along_axis(row, cols, axis=1)
             value = jnp.where(value < 0, -1, value + first * LANES)
             place = jnp.where(rows == first + k, value, place)
-        slot_ids[level] = place
+        return place
+
+    def translate(level, source):
+        slot_ids[level] = placed(slot_ids[level], source, their_ranks.at[source])
+
+    def finish(n):
+        a, b = joined[n]
+        ids = placed(near_ids[n], a, far_ranks.at[n])
+        rows, cols = ids >> 7, ids & (LANES - 1)
+        here = [rows == OWN + a * SLOTS + k for k in range(LIVE)]
+        copies[b].wait_recv()
+        far_copies[n].wait_recv()
+        pad = jnp.zeros((8 - LIVE, LANES), jnp.float32)
+        for c in range(COMPS):
+            spots = pl.ds(level_start(b) + c, LIVE, stride=COMPS)
+            value = jnp.concatenate([table[spots, :], pad], axis=0)
+            for k in range(LIVE):
+                row = row8(far_cells[n, k * COMPS + c : k * COMPS + c + 1, :])
+                value = jnp.where(here[k], jnp.take_along_axis(row, cols, axis=1), value)
+            table[spots, :] = value[:LIVE]
 
     def stage(level, found):
         for c in range(COMPS):
@@ -238,6 +267,27 @@
         )
         for level in range(levels - 1)
     ]
+    far_copies, far_small = [], []
+    for n, step in enumerate(joined):
+        for which, (src, dst, peer) in enumerate(
+            (
+                (sent.at[step[0]], far_cells.at[n], far_peers[n]),
+                (ranks.at[step[0]], far_ranks.at[n], far_peers[n]),
+                (ids_out.at[n], near_ids.at[n], partners[step[1]]),
+            )
+        ):
+            copy = pltpu.make_async_remote_copy(
+                src_ref=src,
+                dst_ref=dst,
+                send_sem=far_send_sem.at[n, which],
+                recv_sem=far_recv_sem.at[n, which],
+                device_id=peer,
+                device_id_type=MESH,
+            )
+            if which == 0:
+                far_copies.append(copy)
+            else:
+                far_small.append(copy)
     body_copies = [
         pltpu.make_async_remote_copy(
             src_ref=bodies_out.at[side],
@@ -261,19 +311,21 @@
     stage(0, pick_own(0))
     loads["pos"].wait()
     loads["mass"].wait()
-    for side in range(2):
-        for block in range(4):
-            listed = jnp.int32(0)
-            for j in range(4):
-                hit = (face_lists[0, side, j] == block) & (j < face_counts[0, side])
-                listed = listed + hit.astype(jnp.int32)
-            kept_mass = jnp.where(listed > 0, mass[block : block + 1, :], 0.0)
-            bodies_out[side, block : block + 1, :] = kept_mass
-        for a in range(3):
+
+    def pack_bodies():
+        for side in range(2):
             for block in range(4):
-                bodies_out[side, 4 + 4 * a + block : 5 + 4 * a + block, :] = pos[
-                    a : a + 1, block * LANES : (block + 1) * LANES
-                ]
+                listed = jnp.int32(0)
+                for j in range(4):
+                    hit = (face_lists[0, side, j] == block) & (j < face_counts[0, side])
+                    listed = listed + hit.astype(jnp.int32)
+                kept_mass = jnp.where(listed > 0, mass[block : block + 1, :], 0.0)
+                bodies_out[side, block : block + 1, :] = kept_mass
+            for a in range(3):
+                for block in range(4):
+                    bodies_out[side, 4 + 4 * a + block : 5 + 4 * a + block, :] = pos[
+                        a : a + 1, block * LANES : (block + 1) * LANES
+                    ]
 
     def spread():
         for a in range(3):
@@ -369,33 +421,69 @@
         spread()
         add_pairs(0, bound(0))
 
-    pl.semaphore_wait(barrier, levels + 2)
+    pl.semaphore_wait(barrier, levels + 2 + len(joined))
     copies[0].start()
-    for copy in rank_copies + body_copies:
+    far = dict((step[0], n) for n, step in enumerate(joined))
+    if 0 in far:
+        far_copies[0].start()
+    for copy in rank_copies + far_small:
+        copy.start()
+    if 0 in far:
+        send(1, pick_own(1))
+    pack_bodies()
+    for copy in body_copies:
         copy.start()
 
     @pl.when(jnp.logical_not(early))
     def _():
         spread()
 
-    for level in range(1, levels):
-        keep(level, pick_own(level))
-    for level in range(levels):
-        if level == 3:
+    known = []
+    for i, step in enumerate(STEPS):
+        for level in STEPS[i + 1] if i + 1 < len(STEPS) else ():
+            found = pick_own(level)
+            for source in known:
+                found = pick_got(level, source, found)
+            keep(level, found)
+        if i == BODIES:
             add_bodies(own_bodies, range(4))
             near(0)
             near(1)
-        add_pairs(bound(level), bound(level + 1))
-        if level < levels - 1:
-            rank_copies[level].wait_recv()
-            for later in range(level + 1, levels):
-                translate(later, level)
-        copies[level].wait_recv()
-        if level < levels - 1:
-            send(level + 1, pick_got(level + 1, level, kept(level + 1)))
-            for later in range(level + 2, levels):
-                keep(later, pick_got(later, level, kept(later)))
-    add_pairs(bound(levels), 8 + 3 * (levels - 1))
+        add_pairs(bound(i), bound(i + 1))
+        n = far.get(step[0])
+        last = step[-1] == levels - 1
+        for level in step:
+            if level < levels - 1:
+                rank_copies[level].wait_recv()
+                for later in range(step[-1] + 1, levels):
+                    translate(later, level)
+        if n is not None:
+            far_small[2 * n].wait_recv()
+            far_small[2 * n + 1].wait_recv()
+            if last:
+                copies[step[0]].wait_recv()
+                add_pairs(bound(i + 1), 8 + 3 * (levels - 1))
+            finish(n)
+        if last:
+            if n is None:
+                copies[step[0]].wait_recv()
+                add_pairs(bound(i + 1), 8 + 3 * (levels - 1))
+            break
+        sources = [step[1]] if n is not None else []
+        ahead = STEPS[i + 1]
+        found = kept(ahead[0])
+        for source in sources:
+            found = pick_got(ahead[0], source, found)
+        copies[step[0]].wait_recv()
+        send(ahead[0], pick_got(ahead[0], step[0], found))
+        if ahead[0] in far:
+            far_copies[far[ahead[0]]].start()
+        for later in ahead[1:]:
+            found = kept(later)
+            for source in step:
+                found = pick_got(later, source, found)
+            send(later, found)
+        known += list(step)
     for block in range(4):
         for g in range(LANES // GROUP):
             cells_step(got_row(levels - 1), range(LIVE), block * LANES + g * GROUP)
@@ -404,19 +492,20 @@
             out_ref[a : a + 1, block * LANES : (block + 1) * LANES] = jnp.sum(
                 turned, axis=0, keepdims=True
             )
-    for copy in copies + rank_copies + body_copies:
+    for copy in copies + rank_copies + far_copies + far_small + body_copies:
         copy.wait_send()
 
 
 def shards(sizes, pos, mass, cm, cc, cq, lists, masks, face_lists, face_counts):
     levels = lists.shape[1]
+    joined = sum(len(step) == 2 for step in STEPS)
     f32, i32 = jnp.float32, jnp.int32
     any_space = pl.BlockSpec(memory_space=pl.ANY)
     smem = pl.BlockSpec(memory_space=pltpu.SMEM)
     dma = pltpu.SemaphoreType.DMA
     return pl.pallas_call(
         functools.partial(kernel, sizes, levels),
-        out_shape=jax.ShapeDtypeStruct(pos.shape, f32),
+        out_shape=pltpu.VMEM(pos.shape, f32),
         in_specs=[any_space] * 7 + [smem] * 2,
         out_specs=pl.BlockSpec(memory_space=pltpu.VMEM),
         scratch_shapes=[
@@ -444,6 +533,12 @@
             dma((levels - 1,)),
             dma((2,)),
             dma((2,)),
+            pltpu.VMEM((joined, BLOCK, LANES), f32),
+            pltpu.VMEM((joined, SLOTS, LANES), i32),
+            pltpu.VMEM((joined, 8, LANES), i32),
+            pltpu.VMEM((joined, 8, LANES), i32),
+            dma((joined, 3)),
+            dma((joined, 3)),
         ],
         compiler_params=pltpu.CompilerParams(collective_id=0, has_side_effects=True),
         name="treecode",

time: 45 us -> 42.3 us (0.940)
  the two profiles are of different devices: /device:TPU:4 before, /device:TPU:256 now
where the time goes in v3:
time: 42.3 us; the launch traced here: 42.1 us
  Pallas kernels  41.5 us (98%)
  local copies, waits for them, and re-layouts  0.6 us (1%)
    pallas_call x1, Pallas kernels, shards(): pl.pallas_call(functools.partial(kernel, sizes, levels), out_shape=pltpu....  41.5 us

profile of v3, /device:TPU:256, one launch (start us, length us, event | category | flops | bytes accessed | tf_op | source)
XLA Modules:
  0.0 42.1 jit_solution(1260060009430332629)
XLA Ops:
  0.0 41.5 %treecode.1 = f32[3,512]{1,0:T(4,128)S(1)} custom-call(f32[3,512]{1,0:T(4,128)} %pos_h.1, f32[4,128]{1,0:T(4,128)} %bitcast.7, f32[16,128]{1,0:T(8,128)} %bitcast.6, f32[3,2048]{1,0:T(4,128)} %cc_h.1, f32[6,2048]{1,0:T(8,128)} %cq_h.1, s32[5,8,128]{2,1,0:T(8,128)} %bitcast.4, s32[5,8,128]{2,1,0:T(8,128)} %bitcast.5, s32[1,2,4]{2,1,0:T(2,128)} %face_lists.1, ...), custom_call_target="tpu_custom_call" | custom-call | tf_op jit(solution)/shard_map/treecode/pallas_call | solution.py:506
  41.5 0.6 %copy.11 = f32[3,512]{1,0:T(4,128)} copy(f32[3,512]{1,0:T(4,128)S(1)} %treecode.1) | data formatting | bytes 12288

commit v4 on v3

--- a/solution.py
+++ b/solution.py
@@ -18,14 +18,12 @@
 BLOCK = 64
 GROUP = 32
 KEEP = 8192
-STEPS = ((0, 1), (2,), (3,), (4,))
-BODIES = 2
+STEPS = ((0, 1), (2, 3), (4,))
 PLAN = (
     (8, 7, 2, 0),
-    (8, 8, 4, 1),
-    (11, 10, 6, 3),
-    (15, 12, 8, 6),
-    (20, 20, 12, 10),
+    (8, 8, 4, 2),
+    (14, 11, 7, 6),
+    (20, 20, 13, 11),
 )
 
 
@@ -445,10 +443,13 @@
             for source in known:
                 found = pick_got(level, source, found)
             keep(level, found)
-        if i == BODIES:
-            add_bodies(own_bodies, range(4))
-            near(0)
-            near(1)
+        if i in (0, len(STEPS) - 1):
+            @pl.when(late < 2 if i == 0 else late >= 2)
+            def _():
+                add_bodies(own_bodies, range(4))
+                near(0)
+                near(1)
+
         add_pairs(bound(i), bound(i + 1))
         n = far.get(step[0])
         last = step[-1] == levels - 1
@@ -463,7 +464,12 @@
             if last:
                 copies[step[0]].wait_recv()
                 add_pairs(bound(i + 1), 8 + 3 * (levels - 1))
-            finish(n)
+            if step[0] > 0 and not last:
+                copies[step[0]].wait_recv()
+                soon = pick_got(STEPS[i + 1][0], step[0], kept(STEPS[i + 1][0]))
+                finish(n)
+            else:
+                finish(n)
         if last:
             if n is None:
                 copies[step[0]].wait_recv()
@@ -471,11 +477,14 @@
             break
         sources = [step[1]] if n is not None else []
         ahead = STEPS[i + 1]
-        found = kept(ahead[0])
-        for source in sources:
-            found = pick_got(ahead[0], source, found)
-        copies[step[0]].wait_recv()
-        send(ahead[0], pick_got(ahead[0], step[0], found))
+        if n is not None and step[0] > 0:
+            send(ahead[0], pick_got(ahead[0], step[1], soon))
+        else:
+            found = kept(ahead[0])
+            for source in sources:
+                found = pick_got(ahead[0], source, found)
+            copies[step[0]].wait_recv()
+            send(ahead[0], pick_got(ahead[0], step[0], found))
         if ahead[0] in far:
             far_copies[far[ahead[0]]].start()
         for later in ahead[1:]:

time: 42.3 us -> 41.3 us (0.976)
  Pallas kernels: 41.5 us -> 40.5 us
    pallas_call x1, Pallas kernels: 41.5 us -> 40.5 us  [shards(): pl.pallas_call(functools.partial(kernel, sizes, levels), out_shape=pltpu....]
where the time goes in v4:
time: 41.3 us; the launch traced here: 41.2 us
  Pallas kernels  40.5 us (98%)
  local copies, waits for them, and re-layouts  0.6 us (1%)
    pallas_call x1, Pallas kernels, shards(): pl.pallas_call(functools.partial(kernel, sizes, levels), out_shape=pltpu....  40.5 us

profile of v4, /device:TPU:256, one launch (start us, length us, event | category | flops | bytes accessed | tf_op | source)
XLA Modules:
  0.0 41.2 jit_solution(2222512296687366590)
XLA Ops:
  0.0 40.5 %treecode.1 = f32[3,512]{1,0:T(4,128)S(1)} custom-call(f32[3,512]{1,0:T(4,128)} %pos_h.1, f32[4,128]{1,0:T(4,128)} %bitcast.7, f32[16,128]{1,0:T(8,128)} %bitcast.6, f32[3,2048]{1,0:T(4,128)} %cc_h.1, f32[6,2048]{1,0:T(8,128)} %cq_h.1, s32[5,8,128]{2,1,0:T(8,128)} %bitcast.4, s32[5,8,128]{2,1,0:T(8,128)} %bitcast.5, s32[1,2,4]{2,1,0:T(2,128)} %face_lists.1, ...), custom_call_target="tpu_custom_call" | custom-call | tf_op jit(solution)/shard_map/treecode/pallas_call | solution.py:515
  40.6 0.6 %copy.11 = f32[3,512]{1,0:T(4,128)} copy(f32[3,512]{1,0:T(4,128)S(1)} %treecode.1) | data formatting | bytes 12288
